TPU v7x, 512 devices: a whole 4x4x16 slice. The times are simulated.
512 devices in a mesh: gx: 8 (over x, core), gy: 8 (over z_hi, y), gz: 8 (over z_lo).
Axes of the slice: x: 4, y: 4, z: 16 (z_hi: 2, z_lo: 8; z = z_hi * 8 + z_lo), core: 2. Of those that a mesh axis runs over, the one named last changes fastest.
Arguments:
- magnet: float32 [3, 32, 256, 2048], P(None, 'gz', 'gx', 'gy'), may hold values from -1 to 1, as said below
- grains: int32 [32, 256, 2048], P('gz', 'gx', 'gy'), may hold values from 0 to 15
- stiffness_table: float32 [16], replicated, may hold values from 0.2 to 1
- saturation_table: float32 [16], replicated, may hold values from 0.6 to 1.4
- kernel_x: bfloat16 [8, 256], replicated, may hold values from -3 to 3
- kernel_y: bfloat16 [8, 2048], replicated, may hold values from -3 to 3
- kernel_z: bfloat16 [8, 32], replicated, may hold values from -3 to 3
- mixing: float32 [8, 3, 3], replicated, may hold values from -1.25 to 1.25
Outputs:
- magnet_next: float32 [3, 32, 256, 2048], P(None, 'gz', 'gx', 'gy')
- demag_field: float32 [16, 3, 128, 1024], P('gz', None, 'gx', 'gy')
Inputs may be any that keep to these rules, and one draw needn't show every extreme that they name: `magnet`: every cell's three components form a unit vector.
All inputs are finite; a program needn't handle non-finite values.
Results may differ from a plain program's by a relative error of at most 0.00085.
The roundings to bfloat16 on the way count: a program that leaves them out, or rounds other values in their place, can miss the bound.
Values may be sent and summed in bfloat16 or wider, within the bound.
No kernel may reach another device: no remote copies, remote signals or barrier semaphores. Data moves between devices by JAX's collectives and lax.ppermute only.
A program may use at most 128 MiB of HBM per device.

v0:
```python
import jax
import jax.numpy as jnp
from jax import lax
from jax.sharding import PartitionSpec as P

SUBSTEPS = 3
time_step = 0.02
damping = 0.3


def with_halo(x, sides, width):
    for axis, dim in sides:
        count, length = (lax.axis_size(axis), x.shape[dim])
        up = [(i, (i + 1) % count) for i in range(count - 1)]
        down = [(j, i) for i, j in up]
        last = lax.slice_in_dim(x, length - width, length, axis=dim)
        leading = lax.slice_in_dim(x, 0, width, axis=dim)
        before = lax.ppermute(last, axis, up)
        after = lax.ppermute(leading, axis, down)
        x = jnp.concatenate([before, x, after], axis=dim)
    return x


def toeplitz_rows(kernel, offset, extent):
    length = kernel.shape[1] // 2
    flipped = kernel[:, ::-1]
    row_ids = offset + jnp.arange(extent, dtype=jnp.int32)
    picked = jax.vmap(
        lambda row_index: lax.dynamic_slice_in_dim(flipped, length - 1 - row_index, length, 1)
    )(row_ids)
    return jnp.transpose(picked, (1, 0, 2))


def interior(values):
    return values[..., 1:-1, 1:-1, 1:-1]


def shifted(values, along, begin_at):
    slicer = [slice(1, -1), slice(1, -1), slice(1, -1)]
    slicer[along] = slice(begin_at, begin_at + values.shape[along - 3] - 2)
    leading = [slice(None)] * (values.ndim - 3)
    return values[tuple(leading + slicer)]


def cross_product(first_vec, second_vec):
    return jnp.stack(
        [
            first_vec[1] * second_vec[2] - first_vec[2] * second_vec[1],
            first_vec[2] * second_vec[0] - first_vec[0] * second_vec[2],
            first_vec[0] * second_vec[1] - first_vec[1] * second_vec[0],
        ]
    )


def exchange_update(magnet_rim, stiff_rim, saturation, demag_fine):
    centre = interior(magnet_rim)
    stiff_centre = interior(stiff_rim)
    coupled = jnp.zeros_like(centre)
    for along in range(3):
        for begin_at in (0, 2):
            stiff_near = shifted(stiff_rim, along, begin_at)
            denominator = stiff_centre + stiff_near
            weight = (
                2.0 * stiff_centre * stiff_near / jnp.where(denominator > 0.0, denominator, 1.0)
            )
            coupled = coupled + weight[None] * (shifted(magnet_rim, along, begin_at) - centre)
    inside = saturation > 0.0
    safe_sat = jnp.where(inside, saturation, 1.0)
    field_total = 2.0 * coupled / safe_sat[None] + demag_fine
    torque = cross_product(centre, field_total)
    raw_next = centre - time_step * (torque + damping * cross_product(centre, torque))
    length_sq = jnp.sqrt(jnp.sum(raw_next * raw_next, axis=0))
    safe_len = jnp.where(inside, length_sq, 1.0)
    return jnp.where(inside[None], raw_next / safe_len[None], 0.0)


def coarsen(magnet, saturation):
    weighted = saturation[None] * magnet
    comps, depth, width, height = weighted.shape
    shaped = weighted.reshape(comps, depth // 2, 2, width // 2, 2, height // 2, 2)
    return jnp.mean(shaped, axis=(2, 4, 6)).astype(jnp.bfloat16)


def prolong(demag):
    moved = jnp.transpose(demag, (1, 0, 2, 3))
    return jnp.repeat(jnp.repeat(jnp.repeat(moved, 2, axis=1), 2, axis=2), 2, axis=3)


def material_field(grains, lookup):
    labels = jnp.arange(lookup.shape[0], dtype=jnp.int32)
    matches = grains[None] == labels[:, None, None, None]
    return jnp.sum(jnp.where(matches, lookup[:, None, None, None], 0.0), axis=0)


def local(magnet, grains, stiffness_table, saturation_table, kernel_x, kernel_y, kernel_z, mixing):
    stiffness = material_field(grains, stiffness_table)
    saturation = material_field(grains, saturation_table)
    coarse = coarsen(magnet, saturation)
    rows_z = coarse.shape[1]
    rows_x = coarse.shape[2]
    rows_y = coarse.shape[3]
    block_x = toeplitz_rows(kernel_x, lax.axis_index("gx") * rows_x, rows_x)
    columns = block_x
    along_x = jnp.einsum(
        "rab,jzby->rjzay",
        columns,
        lax.all_gather(coarse, "gx", axis=2, tiled=True),
        preferred_element_type=jnp.float32,
    ).astype(jnp.bfloat16)
    block_y = toeplitz_rows(kernel_y, lax.axis_index("gy") * rows_y, rows_y)
    columns = block_y
    along_y = jnp.einsum(
        "rby,rjzxy->rjzxb",
        columns,
        lax.all_gather(along_x, "gy", axis=4, tiled=True),
        preferred_element_type=jnp.float32,
    ).astype(jnp.bfloat16)
    whole_z = toeplitz_rows(kernel_z, 0, kernel_z.shape[1] // 2).astype(jnp.float32)
    offset = lax.axis_index("gz") * rows_z
    own_rows = lax.dynamic_slice_in_dim(whole_z, offset, rows_z, 1)
    weights = jnp.einsum("rij,raz->airjz", mixing, own_rows, precision=lax.Precision.HIGHEST)
    columns = weights
    demag = jnp.einsum(
        "airjz,rjzxy->aixy",
        columns,
        lax.all_gather(along_y, "gz", axis=2, tiled=True).astype(jnp.float32),
        precision=lax.Precision.HIGHEST,
    )
    demag_fine = prolong(demag)
    stiff_rim = with_halo(
        stiffness[None].astype(jnp.bfloat16), (("gx", 2), ("gy", 3), ("gz", 1)), 1
    ).astype(jnp.float32)[0]
    state = magnet
    for substep in range(SUBSTEPS):
        magnet_rim = with_halo(state, (("gx", 2), ("gy", 3), ("gz", 1)), 1)
        state = exchange_update(magnet_rim, stiff_rim, saturation, demag_fine)
    return (state, demag)


def solution(mesh):
    in_specs = (P(None, "gz", "gx", "gy"), P("gz", "gx", "gy"), P(), P(), P(), P(), P(), P())
    out_specs = (P(None, "gz", "gx", "gy"), P("gz", None, "gx", "gy"))
    return jax.shard_map(local, mesh=mesh, in_specs=in_specs, out_specs=out_specs, check_vma=False)
```

profile of v0, /device:TPU:320, one launch (start us, length us, event | category | flops | bytes accessed | tf_op | source)
XLA Modules:
  0.0 573.6 jit_solution(10090580710956281949)
XLA Ops:
  9.6 26.6 %reshape.132 = f32[3,2,2,16,2,128,2]{6,5,4,3,2,1,0:T(8,128)} reshape(f32[3,4,32,256]{3,2,1,0:T(8,128)S(1)} %broadcast_multiply_fusion) | data formatting | bytes 786432 | tf_op jit(solution)/shard_map/reshape | solution.py:80
  36.2 9.5 %reduce_sum.56 = f32[3,2,16,128]{3,2,1,0:T(8,128)S(1)} reduce(f32[3,2,2,16,2,128,2]{6,5,4,3,2,1,0:T(8,128)} %reshape.132, f32[]{:T(128)} %constant.19.clone.1), dimensions={2,4,6}, to_apply=%region_2.3 | reduce | flops 86016 | bytes 442372 | tf_op jit(solution)/shard_map/reduce_sum | solution.py:81
  45.6 13.2 %all_gather.9 = bf16[3,2,128,128]{3,2,1,0:T(8,128)(2,1)S(1)} all-gather(bf16[3,2,16,128]{3,2,1,0:T(8,128)(2,1)S(1)} %multiply_convert_fusion), channel_id=1, replica_groups=mesh['gx'=8,'gy'=8,'gz'=8] {'gx'}, dimensions={2}, use_global_device_ids=true | all-gather | bytes 221184 | tf_op jit(solution)/shard_map/all_gather | solution.py:107
  59.0 21.6 %while.4 = (s32[]{:T(128)}, bf16[8,256]{1,0:T(8,128)(2,1)S(1)}, s32[16,2]{0,1:T(2,128)S(1)}, bf16[16,8,128]{2,1,0:T(8,128)(2,1)S(1)}, s32[]{:T(128)}) while((s32[]{:T(128)}, bf16[8,256]{1,0:T(8,128)(2,1)S(1)}, s32[16,2]{0,1:T(2,128)S(1)}, bf16[16,8,128]{2,1,0:T(8,128)(2,1)S(1)}, s32[]{:T(128)}) %tuple.89), condition=%wide.while_cond.1, body=%wide.while_body.1.sunk | while | flops 2 | bytes 4201 | solution.py:29
  92.1 252.3 %while.5 = (s32[]{:T(128)}, bf16[8,2048]{1,0:T(8,128)(2,1)S(1)}, s32[128,2]{0,1:T(2,128)S(1)}, bf16[128,8,1024]{2,1,0:T(8,128)(2,1)}, s32[]{:T(128)}) while((s32[]{:T(128)}, bf16[8,2048]{1,0:T(8,128)(2,1)S(1)}, s32[128,2]{0,1:T(2,128)S(1)}, bf16[128,8,1024]{2,1,0:T(8,128)(2,1)}, s32[]{:T(128)}) %tuple.86), condition=%wide.while_cond.2, body=%wide.while_body.2.sunk | while | flops 2 | bytes 33381 | solution.py:29
  344.5 21.9 %while.3 = (s32[]{:T(128)}, bf16[8,32]{1,0:T(8,128)(2,1)S(1)}, s32[16,2]{0,1:T(2,128)S(1)}, bf16[16,8,16]{2,1,0:T(8,128)(2,1)S(1)}, s32[]{:T(128)}) while((s32[]{:T(128)}, bf16[8,32]{1,0:T(8,128)(2,1)S(1)}, s32[16,2]{0,1:T(2,128)S(1)}, bf16[16,8,16]{2,1,0:T(8,128)(2,1)S(1)}, s32[]{:T(128)}) %tuple.92), condition=%wide.while_cond, body=%wide.while_body.sunk | while | flops 2 | bytes 4201 | solution.py:29
  366.4 4.2 fusion.6
  376.9 14.6 %collective-permute-done.2 = bf16[1,4,34,1]{3,1,2,0:T(4,128)(2,1)S(1)} collective-permute-done((bf16[1,4,34,1]{3,1,2,0:T(4,128)(2,1)S(1)}, bf16[1,4,34,1]{3,1,2,0:T(4,128)(2,1)S(1)}, u32[]{:S(2)}, u32[]{:S(2)}) %collective-permute-start.2) | collective-permute-done | bytes 304 | tf_op jit(solution)/shard_map/ppermute | solution.py:18
  394.1 3.9 collective-permute-start.8
  400.1 3.9 collective-permute-start.4
  404.1 7.6 %collective-permute-done.9 = f32[3,4,34,1]{3,1,2,0:T(4,128)S(1)} collective-permute-done((f32[3,4,34,1]{3,1,2,0:T(4,128)S(1)}, f32[3,4,34,1]{3,1,2,0:T(4,128)S(1)}, u32[]{:S(2)}, u32[]{:S(2)}) %collective-permute-start.9) | collective-permute-done | bytes 1664 | tf_op jit(solution)/shard_map/ppermute | solution.py:19
  411.7 15.3 %collective-permute-done.8 = f32[3,4,34,1]{3,1,2,0:T(4,128)S(1)} collective-permute-done((f32[3,4,34,1]{3,1,2,0:T(4,128)S(1)}, f32[3,4,34,1]{3,1,2,0:T(4,128)S(1)}, u32[]{:S(2)}, u32[]{:S(2)}) %collective-permute-start.8) | collective-permute-done | bytes 1664 | tf_op jit(solution)/shard_map/ppermute | solution.py:18
  428.4 12.6 %collective-permute-start.11 = (f32[3,1,34,258]{3,2,1,0:T(8,128)}, f32[3,1,34,258]{3,2,1,0:T(8,128)}, u32[]{:S(2)}, u32[]{:S(2)}) collective-permute-start(f32[3,1,34,258]{3,2,1,0:T(8,128)} %get-tuple-element.96), channel_id=1, source_target_pairs={{1,0},{2,1},{3,2},{4,3},{5,4},{6,5},{7,6},{9,8},{10,9},{11,10},{12... | collective-permute-start | bytes 315800 | tf_op jit(solution)/shard_map/ppermute | solution.py:19
  457.9 4.2 collective-permute-done.13
  464.6 3.6 collective-permute-start.14
  470.8 13.5 %collective-permute-done.14 = f32[3,4,34,1]{3,1,2,0:T(4,128)S(1)} collective-permute-done((f32[3,4,34,1]{3,1,2,0:T(4,128)S(1)}, f32[3,4,34,1]{3,1,2,0:T(4,128)S(1)}, u32[]{:S(2)}, u32[]{:S(2)}) %collective-permute-start.14) | collective-permute-done | bytes 1664 | tf_op jit(solution)/shard_map/ppermute | solution.py:18
  484.9 16.8 %collective-permute-start.17 = (f32[3,1,34,258]{3,2,1,0:T(8,128)S(1)}, f32[3,1,34,258]{3,2,1,0:T(8,128)S(1)}, u32[]{:S(2)}, u32[]{:S(2)}) collective-permute-start(f32[3,1,34,258]{3,2,1,0:T(8,128)S(1)} %get-tuple-element.94), channel_id=1, source_target_pairs={{1,0},{2,1},{3,2},{4,3},{5,4},{6,5},{7,6},{9,8},{10,9},{11,10},{12... | collective-permute-start | bytes 315800 | tf_op jit(solution)/shard_map/ppermute | solution.py:19
  506.0 4.1 collective-permute-done.16
  514.2 4.1 collective-permute-done.19
  520.4 3.9 collective-permute-start.20
  525.0 4.0 collective-permute-done.21
  529.0 15.4 %collective-permute-done.20 = f32[3,4,34,1]{3,1,2,0:T(4,128)S(1)} collective-permute-done((f32[3,4,34,1]{3,1,2,0:T(4,128)S(1)}, f32[3,4,34,1]{3,1,2,0:T(4,128)S(1)}, u32[]{:S(2)}, u32[]{:S(2)}) %collective-permute-start.20) | collective-permute-done | bytes 1664 | tf_op jit(solution)/shard_map/ppermute | solution.py:18
  545.0 11.7 %collective-permute-start.23 = (f32[3,1,34,258]{3,2,1,0:T(8,128)S(1)}, f32[3,1,34,258]{3,2,1,0:T(8,128)S(1)}, u32[]{:S(2)}, u32[]{:S(2)}) collective-permute-start(f32[3,1,34,258]{3,2,1,0:T(8,128)S(1)} %get-tuple-element.92), channel_id=1, source_target_pairs={{1,0},{2,1},{3,2},{4,3},{5,4},{6,5},{7,6},{9,8},{10,9},{11,10},{12... | collective-permute-start | bytes 315800 | tf_op jit(solution)/shard_map/ppermute | solution.py:19
  560.8 4.1 collective-permute-done.22
  (637 shorter events, 361.7 us)
Async XLA Ops:
  7.2 359.3 %all-gather.3.cloned.1.call-start = ((), (), s32[]{:S(2)}) async-start(), calls=%async_computation | async-start | bytes 1769472 | tf_op jit(solution)/shard_map/all_gather | solution.py:115
  81.5 364.0 %all-gather.5.cloned.1.call-start = ((), (), s32[]{:S(2)}) async-start(), calls=%async_computation.1 | async-start | bytes 1769472 | tf_op jit(solution)/shard_map/all_gather | solution.py:126
  81.6 310.4 %collective-permute-start.7 = (f32[3,4,1,256]{3,1,2,0:T(4,128)S(1)}, f32[3,4,1,256]{3,1,2,0:T(4,128)S(1)}, u32[]{:S(2)}, u32[]{:S(2)}) collective-permute-start(f32[3,4,1,256]{3,1,2,0:T(4,128)S(1)} %copy.552), channel_id=1, source_target_pairs={{64,0},{128,64},{192,128},{256,192},{320,256},{384,320},{448,384},... | collective-permute-start | bytes 36872 | tf_op jit(solution)/shard_map/ppermute | solution.py:19
  82.9 308.8 %collective-permute-start.6 = (f32[3,4,1,256]{3,1,2,0:T(4,128)S(1)}, f32[3,4,1,256]{3,1,2,0:T(4,128)S(1)}, u32[]{:S(2)}, u32[]{:S(2)}) collective-permute-start(f32[3,4,1,256]{3,1,2,0:T(4,128)S(1)} %copy.553), channel_id=1, source_target_pairs={{0,64},{64,128},{128,192},{192,256},{256,320},{320,384},{384,448},... | collective-permute-start | bytes 36872 | tf_op jit(solution)/shard_map/ppermute | solution.py:18
  86.0 284.7 %collective-permute-start = (bf16[1,4,1,256]{3,2,1,0:T(2,128)(2,1)S(1)}, bf16[1,4,1,256]{3,2,1,0:T(2,128)(2,1)S(1)}, u32[]{:S(2)}, u32[]{:S(2)}) collective-permute-start(bf16[1,4,1,256]{3,2,1,0:T(2,128)(2,1)S(1)} %get-tuple-element.126), channel_id=1, source_target_pairs={{0,64},{64,128},{128,192},{192,256},{256,320},{320,384},{384,448},... | collective-permute-start | bytes 6152 | tf_op jit(solution)/shard_map/ppermute | solution.py:18
  89.5 281.3 %collective-permute-start.1 = (bf16[1,4,1,256]{3,2,1,0:T(2,128)(2,1)S(1)}, bf16[1,4,1,256]{3,2,1,0:T(2,128)(2,1)S(1)}, u32[]{:S(2)}, u32[]{:S(2)}) collective-permute-start(bf16[1,4,1,256]{3,2,1,0:T(2,128)(2,1)S(1)} %get-tuple-element.125), channel_id=1, source_target_pairs={{64,0},{128,64},{192,128},{256,192},{320,256},{384,320},{448,384},... | collective-permute-start | bytes 6152 | tf_op jit(solution)/shard_map/ppermute | solution.py:19
  370.9 6.0 %collective-permute-start.3 = (bf16[1,4,34,1]{3,1,2,0:T(4,128)(2,1)S(1)}, bf16[1,4,34,1]{3,1,2,0:T(4,128)(2,1)S(1)}, u32[]{:S(2)}, u32[]{:S(2)}) collective-permute-start(bf16[1,4,34,1]{3,1,2,0:T(4,128)(2,1)S(1)} %get-tuple-element.124), channel_id=1, source_target_pairs={{8,0},{16,8},{24,16},{32,24},{40,32},{48,40},{56,48},{9,1},{17,9},... | collective-permute-start | bytes 824 | tf_op jit(solution)/shard_map/ppermute | solution.py:19
  374.0 17.5 %collective-permute-start.2 = (bf16[1,4,34,1]{3,1,2,0:T(4,128)(2,1)S(1)}, bf16[1,4,34,1]{3,1,2,0:T(4,128)(2,1)S(1)}, u32[]{:S(2)}, u32[]{:S(2)}) collective-permute-start(bf16[1,4,34,1]{3,1,2,0:T(4,128)(2,1)S(1)} %get-tuple-element.123), channel_id=1, source_target_pairs={{0,8},{8,16},{16,24},{24,32},{32,40},{40,48},{48,56},{1,9},{9,17},... | collective-permute-start | bytes 824 | tf_op jit(solution)/shard_map/ppermute | solution.py:18
  392.2 19.5 %collective-permute-start.9 = (f32[3,4,34,1]{3,1,2,0:T(4,128)S(1)}, f32[3,4,34,1]{3,1,2,0:T(4,128)S(1)}, u32[]{:S(2)}, u32[]{:S(2)}) collective-permute-start(f32[3,4,34,1]{3,1,2,0:T(4,128)S(1)} %get-tuple-element.108), channel_id=1, source_target_pairs={{8,0},{16,8},{24,16},{32,24},{40,32},{48,40},{56,48},{9,1},{17,9},... | collective-permute-start | bytes 4904 | tf_op jit(solution)/shard_map/ppermute | solution.py:19
  394.1 32.9 %collective-permute-start.8 = (f32[3,4,34,1]{3,1,2,0:T(4,128)S(1)}, f32[3,4,34,1]{3,1,2,0:T(4,128)S(1)}, u32[]{:S(2)}, u32[]{:S(2)}) collective-permute-start(f32[3,4,34,1]{3,1,2,0:T(4,128)S(1)} %get-tuple-element.107), channel_id=1, source_target_pairs={{0,8},{8,16},{16,24},{24,32},{32,40},{40,48},{48,56},{1,9},{9,17},... | collective-permute-start | bytes 4904 | tf_op jit(solution)/shard_map/ppermute | solution.py:18
  398.2 46.2 %collective-permute-start.5 = (bf16[1,1,34,258]{3,2,1,0:T(8,128)(2,1)S(1)}, bf16[1,1,34,258]{3,2,1,0:T(8,128)(2,1)S(1)}, u32[]{:S(2)}, u32[]{:S(2)}) collective-permute-start(bf16[1,1,34,258]{3,2,1,0:T(8,128)(2,1)S(1)} %copy.554), channel_id=1, source_target_pairs={{1,0},{2,1},{3,2},{4,3},{5,4},{6,5},{7,6},{9,8},{10,9},{11,10},{12... | collective-permute-start | bytes 52640 | tf_op jit(solution)/shard_map/ppermute | solution.py:19
  400.1 44.3 %collective-permute-start.4 = (bf16[1,1,34,258]{3,2,1,0:T(8,128)(2,1)S(1)}, bf16[1,1,34,258]{3,2,1,0:T(8,128)(2,1)S(1)}, u32[]{:S(2)}, u32[]{:S(2)}) collective-permute-start(bf16[1,1,34,258]{3,2,1,0:T(8,128)(2,1)S(1)} %copy.555), channel_id=1, source_target_pairs={{0,1},{1,2},{2,3},{3,4},{4,5},{5,6},{6,7},{8,9},{9,10},{10,11},{11... | collective-permute-start | bytes 52640 | tf_op jit(solution)/shard_map/ppermute | solution.py:18
  428.4 24.0 %collective-permute-start.11 = (f32[3,1,34,258]{3,2,1,0:T(8,128)}, f32[3,1,34,258]{3,2,1,0:T(8,128)}, u32[]{:S(2)}, u32[]{:S(2)}) collective-permute-start(f32[3,1,34,258]{3,2,1,0:T(8,128)} %get-tuple-element.96), channel_id=1, source_target_pairs={{1,0},{2,1},{3,2},{4,3},{5,4},{6,5},{7,6},{9,8},{10,9},{11,10},{12... | collective-permute-start | bytes 315800 | tf_op jit(solution)/shard_map/ppermute | solution.py:19
  441.0 11.4 %collective-permute-start.10 = (f32[3,1,34,258]{3,2,1,0:T(8,128)}, f32[3,1,34,258]{3,2,1,0:T(8,128)}, u32[]{:S(2)}, u32[]{:S(2)}) collective-permute-start(f32[3,1,34,258]{3,2,1,0:T(8,128)} %get-tuple-element.95), channel_id=1, source_target_pairs={{0,1},{1,2},{2,3},{3,4},{4,5},{5,6},{6,7},{8,9},{9,10},{10,11},{11... | collective-permute-start | bytes 315800 | tf_op jit(solution)/shard_map/ppermute | solution.py:18
  456.1 6.0 %collective-permute-start.13 = (f32[3,4,1,256]{3,1,2,0:T(4,128)S(1)}, f32[3,4,1,256]{3,1,2,0:T(4,128)S(1)}, u32[]{:S(2)}, u32[]{:S(2)}) collective-permute-start(f32[3,4,1,256]{3,1,2,0:T(4,128)S(1)} %copy.455), channel_id=1, source_target_pairs={{64,0},{128,64},{192,128},{256,192},{320,256},{384,320},{448,384},... | collective-permute-start | bytes 36872 | tf_op jit(solution)/shard_map/ppermute | solution.py:19
  462.3 8.5 %collective-permute-start.15 = (f32[3,4,34,1]{3,1,2,0:T(4,128)S(1)}, f32[3,4,34,1]{3,1,2,0:T(4,128)S(1)}, u32[]{:S(2)}, u32[]{:S(2)}) collective-permute-start(f32[3,4,34,1]{3,1,2,0:T(4,128)S(1)} %get-tuple-element.104), channel_id=1, source_target_pairs={{8,0},{16,8},{24,16},{32,24},{40,32},{48,40},{56,48},{9,1},{17,9},... | collective-permute-start | bytes 4904 | tf_op jit(solution)/shard_map/ppermute | solution.py:19
  464.6 19.7 %collective-permute-start.14 = (f32[3,4,34,1]{3,1,2,0:T(4,128)S(1)}, f32[3,4,34,1]{3,1,2,0:T(4,128)S(1)}, u32[]{:S(2)}, u32[]{:S(2)}) collective-permute-start(f32[3,4,34,1]{3,1,2,0:T(4,128)S(1)} %get-tuple-element.103), channel_id=1, source_target_pairs={{0,8},{8,16},{16,24},{24,32},{32,40},{40,48},{48,56},{1,9},{9,17},... | collective-permute-start | bytes 4904 | tf_op jit(solution)/shard_map/ppermute | solution.py:18
  484.9 21.1 %collective-permute-start.17 = (f32[3,1,34,258]{3,2,1,0:T(8,128)S(1)}, f32[3,1,34,258]{3,2,1,0:T(8,128)S(1)}, u32[]{:S(2)}, u32[]{:S(2)}) collective-permute-start(f32[3,1,34,258]{3,2,1,0:T(8,128)S(1)} %get-tuple-element.94), channel_id=1, source_target_pairs={{1,0},{2,1},{3,2},{4,3},{5,4},{6,5},{7,6},{9,8},{10,9},{11,10},{12... | collective-permute-start | bytes 315800 | tf_op jit(solution)/shard_map/ppermute | solution.py:19
  501.7 8.5 %collective-permute-start.16 = (f32[3,1,34,258]{3,2,1,0:T(8,128)S(1)}, f32[3,1,34,258]{3,2,1,0:T(8,128)S(1)}, u32[]{:S(2)}, u32[]{:S(2)}) collective-permute-start(f32[3,1,34,258]{3,2,1,0:T(8,128)S(1)} %get-tuple-element.93), channel_id=1, source_target_pairs={{0,1},{1,2},{2,3},{3,4},{4,5},{5,6},{6,7},{8,9},{9,10},{10,11},{11... | collective-permute-start | bytes 315800 | tf_op jit(solution)/shard_map/ppermute | solution.py:18
  512.6 5.7 %collective-permute-start.19 = (f32[3,4,1,256]{3,1,2,0:T(4,128)S(1)}, f32[3,4,1,256]{3,1,2,0:T(4,128)S(1)}, u32[]{:S(2)}, u32[]{:S(2)}) collective-permute-start(f32[3,4,1,256]{3,1,2,0:T(4,128)S(1)} %copy.469), channel_id=1, source_target_pairs={{64,0},{128,64},{192,128},{256,192},{320,256},{384,320},{448,384},... | collective-permute-start | bytes 36872 | tf_op jit(solution)/shard_map/ppermute | solution.py:19
  518.5 10.5 %collective-permute-start.21 = (f32[3,4,34,1]{3,1,2,0:T(4,128)S(1)}, f32[3,4,34,1]{3,1,2,0:T(4,128)S(1)}, u32[]{:S(2)}, u32[]{:S(2)}) collective-permute-start(f32[3,4,34,1]{3,1,2,0:T(4,128)S(1)} %get-tuple-element.100), channel_id=1, source_target_pairs={{8,0},{16,8},{24,16},{32,24},{40,32},{48,40},{56,48},{9,1},{17,9},... | collective-permute-start | bytes 4904 | tf_op jit(solution)/shard_map/ppermute | solution.py:19
  520.4 24.0 %collective-permute-start.20 = (f32[3,4,34,1]{3,1,2,0:T(4,128)S(1)}, f32[3,4,34,1]{3,1,2,0:T(4,128)S(1)}, u32[]{:S(2)}, u32[]{:S(2)}) collective-permute-start(f32[3,4,34,1]{3,1,2,0:T(4,128)S(1)} %get-tuple-element.99), channel_id=1, source_target_pairs={{0,8},{8,16},{16,24},{24,32},{32,40},{40,48},{48,56},{1,9},{9,17},... | collective-permute-start | bytes 4904 | tf_op jit(solution)/shard_map/ppermute | solution.py:18
  545.0 15.8 %collective-permute-start.23 = (f32[3,1,34,258]{3,2,1,0:T(8,128)S(1)}, f32[3,1,34,258]{3,2,1,0:T(8,128)S(1)}, u32[]{:S(2)}, u32[]{:S(2)}) collective-permute-start(f32[3,1,34,258]{3,2,1,0:T(8,128)S(1)} %get-tuple-element.92), channel_id=1, source_target_pairs={{1,0},{2,1},{3,2},{4,3},{5,4},{6,5},{7,6},{9,8},{10,9},{11,10},{12... | collective-permute-start | bytes 315800 | tf_op jit(solution)/shard_map/ppermute | solution.py:19
  556.7 8.3 %collective-permute-start.22 = (f32[3,1,34,258]{3,2,1,0:T(8,128)S(1)}, f32[3,1,34,258]{3,2,1,0:T(8,128)S(1)}, u32[]{:S(2)}, u32[]{:S(2)}) collective-permute-start(f32[3,1,34,258]{3,2,1,0:T(8,128)S(1)} %get-tuple-element.91), channel_id=1, source_target_pairs={{0,1},{1,2},{2,3},{3,4},{4,5},{5,6},{6,7},{8,9},{9,10},{10,11},{11... | collective-permute-start | bytes 315800 | tf_op jit(solution)/shard_map/ppermute | solution.py:18
  (13 other events, 562.1 us)
Sparse Core Ops, SparseCore 0:
  81.6 92.3 all-gather.2
  370.8 70.4 all-gather.4
where the time goes:
time: 576 us; the launch traced here: 574 us
  local copies, waits for them, and re-layouts  331 us (57%)
  waiting for transfers between devices  93.2 us (16%)
  starting transfers between devices  90.5 us (16%)
  other arithmetic  22.3 us (4%)
  between operations  14.9 us (3%)
  blocking collectives  13.2 us (2%)
  matrix products  7.96 us (1%)
    gather x480, local copies, waits for them, and re-layouts  296 us
    ppermute x12, waiting for transfers between devices, with_halo(): before = lax.ppermute(last, axis, up)  67 us
    ppermute x12, starting transfers between devices, with_halo(): after = lax.ppermute(leading, axis, down)  57.4 us
    ppermute x12, starting transfers between devices, with_halo(): before = lax.ppermute(last, axis, up)  33 us
    reshape x1, local copies, waits for them, and re-layouts, coarsen(): weighted.reshape(comps, depth // 2, 2, width // 2, 2, height // 2, 2)  26.6 us
    ppermute x12, waiting for transfers between devices, with_halo(): after = lax.ppermute(leading, axis, down)  26.1 us
    all_gather x1, blocking collectives, local(): lax.all_gather(coarse, 'gx', axis=2, tiled=True)  13.2 us
  transfers between devices with their start and end apart: 26, of which 14 were waited for; matrix products, arithmetic and copies ran while one was open for 51% of the time, Pallas kernels for 0%

commit v1 on v0

--- a/solution.py
+++ b/solution.py
@@ -6,6 +6,18 @@
 SUBSTEPS = 3
 time_step = 0.02
 damping = 0.3
+
+
+def threads_treat(local_x):
+    return jnp.concatenate(
+        lax.all_to_all(
+            jnp.stack(tuple((local_x for _ in range(lax.axis_size("gx")))), axis=0),
+            "gx",
+            split_axis=0,
+            concat_axis=0,
+        ),
+        2,
+    )
 
 
 def with_halo(x, sides, width):
@@ -102,10 +114,7 @@
     block_x = toeplitz_rows(kernel_x, lax.axis_index("gx") * rows_x, rows_x)
     columns = block_x
     along_x = jnp.einsum(
-        "rab,jzby->rjzay",
-        columns,
-        lax.all_gather(coarse, "gx", axis=2, tiled=True),
-        preferred_element_type=jnp.float32,
+        "rab,jzby->rjzay", columns, threads_treat(coarse), preferred_element_type=jnp.float32
     ).astype(jnp.bfloat16)
     block_y = toeplitz_rows(kernel_y, lax.axis_index("gy") * rows_y, rows_y)
     columns = block_y

time: 576 us -> 641 us (1.11)
  the two profiles are of different devices: /device:TPU:320 before, /device:TPU:322 now
where the time goes in v1:
time: 641 us; the launch traced here: 638 us
  local copies, waits for them, and re-layouts  330 us (51%)
  waiting for transfers between devices  157 us (24%)
  starting transfers between devices  106 us (17%)
  other arithmetic  22.3 us (3%)
  between operations  14.9 us (2%)
  matrix products  7.97 us (1%)
    gather x480, local copies, waits for them, and re-layouts  294 us
    all_gather x1, waiting for transfers between devices, local(): lax.all_gather(along_x, 'gy', axis=4, tiled=True)  70 us
    ppermute x12, starting transfers between devices, with_halo(): after = lax.ppermute(leading, axis, down)  68.7 us
    ppermute x12, waiting for transfers between devices, with_halo(): before = lax.ppermute(last, axis, up)  67.2 us
    ppermute x12, starting transfers between devices, with_halo(): before = lax.ppermute(last, axis, up)  32.1 us
    reshape x1, local copies, waits for them, and re-layouts, coarsen(): weighted.reshape(comps, depth // 2, 2, width // 2, 2, height // 2, 2)  26.5 us
    ppermute x12, waiting for transfers between devices, with_halo(): after = lax.ppermute(leading, axis, down)  19.6 us
  transfers between devices with their start and end apart: 27, of which 14 were waited for; matrix products, arithmetic and copies ran while one was open for 49% of the time, Pallas kernels for 0%

profile of v1, /device:TPU:322, one launch (start us, length us, event | category | flops | bytes accessed | tf_op | source)
XLA Modules:
  0.0 638.2 jit_solution(877827879802203518)
XLA Ops:
  9.5 26.5 %reshape.140 = f32[3,2,2,16,2,128,2]{6,5,4,3,2,1,0:T(8,128)} reshape(f32[3,4,32,256]{3,2,1,0:T(8,128)S(1)} %broadcast_multiply_fusion) | data formatting | bytes 786432 | tf_op jit(solution)/shard_map/reshape | solution.py:92
  36.1 9.4 %reduce_sum.56 = f32[3,2,16,128]{3,2,1,0:T(8,128)S(1)} reduce(f32[3,2,2,16,2,128,2]{6,5,4,3,2,1,0:T(8,128)} %reshape.140, f32[]{:T(128)} %constant.19.clone.1), dimensions={2,4,6}, to_apply=%region_2.3 | reduce | flops 86016 | bytes 442372 | tf_op jit(solution)/shard_map/reduce_sum | solution.py:93
  46.3 4.8 all-to-all-start
  62.4 249.4 %while.5 = (s32[]{:T(128)}, bf16[8,2048]{1,0:T(8,128)(2,1)S(1)}, s32[128,2]{0,1:T(2,128)S(1)}, bf16[128,8,1024]{2,1,0:T(8,128)(2,1)}, s32[]{:T(128)}) while((s32[]{:T(128)}, bf16[8,2048]{1,0:T(8,128)(2,1)S(1)}, s32[128,2]{0,1:T(2,128)S(1)}, bf16[128,8,1024]{2,1,0:T(8,128)(2,1)}, s32[]{:T(128)}) %tuple.86), condition=%wide.while_cond.2, body=%wide.while_body.2.sunk | while | flops 2 | bytes 33381 | solution.py:41
  312.0 21.7 %while.4 = (s32[]{:T(128)}, bf16[8,256]{1,0:T(8,128)(2,1)S(1)}, s32[16,2]{0,1:T(2,128)S(1)}, bf16[16,8,128]{2,1,0:T(8,128)(2,1)S(1)}, s32[]{:T(128)}) while((s32[]{:T(128)}, bf16[8,256]{1,0:T(8,128)(2,1)S(1)}, s32[16,2]{0,1:T(2,128)S(1)}, bf16[16,8,128]{2,1,0:T(8,128)(2,1)S(1)}, s32[]{:T(128)}) %tuple.89), condition=%wide.while_cond.1, body=%wide.while_body.1.sunk | while | flops 2 | bytes 4201 | solution.py:41
  334.7 23.1 %while.3 = (s32[]{:T(128)}, bf16[8,32]{1,0:T(8,128)(2,1)S(1)}, s32[16,2]{0,1:T(2,128)S(1)}, bf16[16,8,16]{2,1,0:T(8,128)(2,1)S(1)}, s32[]{:T(128)}) while((s32[]{:T(128)}, bf16[8,32]{1,0:T(8,128)(2,1)S(1)}, s32[16,2]{0,1:T(2,128)S(1)}, bf16[16,8,16]{2,1,0:T(8,128)(2,1)S(1)}, s32[]{:T(128)}) %tuple.92), condition=%wide.while_cond, body=%wide.while_body.sunk | while | flops 2 | bytes 4201 | solution.py:41
  357.9 70.0 %all-gather.3.cloned.1.call-done = bf16[8,3,2,16,1024]{4,3,0,2,1:T(8,128)(2,1)} async-done(((bf16[8,3,2,16,128]{4,3,0,2,1:T(8,128)(2,1)}), bf16[8,3,2,16,1024]{4,3,0,2,1:T(8,128)(2,1)}) %all-gather.3.cloned.1.call-update) | async-done | bytes 1572880 | tf_op jit(solution)/shard_map/all_gather | solution.py:124
  427.8 4.2 fusion.6
  432.3 7.6 %collective-permute-start.3 = (bf16[1,4,34,1]{3,1,2,0:T(4,128)(2,1)S(1)}, bf16[1,4,34,1]{3,1,2,0:T(4,128)(2,1)S(1)}, u32[]{:S(2)}, u32[]{:S(2)}) collective-permute-start(bf16[1,4,34,1]{3,1,2,0:T(4,128)(2,1)S(1)} %get-tuple-element.124), channel_id=1, source_target_pairs={{8,0},{16,8},{24,16},{32,24},{40,32},{48,40},{56,48},{9,1},{17,9},... | collective-permute-start | bytes 824 | tf_op jit(solution)/shard_map/ppermute | solution.py:31
  441.9 16.2 %collective-permute-done.2 = bf16[1,4,34,1]{3,1,2,0:T(4,128)(2,1)S(1)} collective-permute-done((bf16[1,4,34,1]{3,1,2,0:T(4,128)(2,1)S(1)}, bf16[1,4,34,1]{3,1,2,0:T(4,128)(2,1)S(1)}, u32[]{:S(2)}, u32[]{:S(2)}) %collective-permute-start.2) | collective-permute-done | bytes 304 | tf_op jit(solution)/shard_map/ppermute | solution.py:30
  460.7 3.9 collective-permute-start.8
  470.7 6.9 %collective-permute-done.9 = f32[3,4,34,1]{3,1,2,0:T(4,128)S(1)} collective-permute-done((f32[3,4,34,1]{3,1,2,0:T(4,128)S(1)}, f32[3,4,34,1]{3,1,2,0:T(4,128)S(1)}, u32[]{:S(2)}, u32[]{:S(2)}) %collective-permute-start.9) | collective-permute-done | bytes 1664 | tf_op jit(solution)/shard_map/ppermute | solution.py:31
  477.6 14.5 %collective-permute-done.8 = f32[3,4,34,1]{3,1,2,0:T(4,128)S(1)} collective-permute-done((f32[3,4,34,1]{3,1,2,0:T(4,128)S(1)}, f32[3,4,34,1]{3,1,2,0:T(4,128)S(1)}, u32[]{:S(2)}, u32[]{:S(2)}) %collective-permute-start.8) | collective-permute-done | bytes 1664 | tf_op jit(solution)/shard_map/ppermute | solution.py:30
  493.5 14.6 %collective-permute-start.11 = (f32[3,1,34,258]{3,2,1,0:T(8,128)}, f32[3,1,34,258]{3,2,1,0:T(8,128)}, u32[]{:S(2)}, u32[]{:S(2)}) collective-permute-start(f32[3,1,34,258]{3,2,1,0:T(8,128)} %get-tuple-element.96), channel_id=1, source_target_pairs={{1,0},{2,1},{3,2},{4,3},{5,4},{6,5},{7,6},{9,8},{10,9},{11,10},{12... | collective-permute-start | bytes 315800 | tf_op jit(solution)/shard_map/ppermute | solution.py:31
  523.8 3.6 collective-permute-start.13
  530.9 4.1 collective-permute-start.14
  538.3 13.0 %collective-permute-done.14 = f32[3,4,34,1]{3,1,2,0:T(4,128)S(1)} collective-permute-done((f32[3,4,34,1]{3,1,2,0:T(4,128)S(1)}, f32[3,4,34,1]{3,1,2,0:T(4,128)S(1)}, u32[]{:S(2)}, u32[]{:S(2)}) %collective-permute-start.14) | collective-permute-done | bytes 1664 | tf_op jit(solution)/shard_map/ppermute | solution.py:30
  552.0 14.2 %collective-permute-start.17 = (f32[3,1,34,258]{3,2,1,0:T(8,128)S(1)}, f32[3,1,34,258]{3,2,1,0:T(8,128)S(1)}, u32[]{:S(2)}, u32[]{:S(2)}) collective-permute-start(f32[3,1,34,258]{3,2,1,0:T(8,128)S(1)} %get-tuple-element.94), channel_id=1, source_target_pairs={{1,0},{2,1},{3,2},{4,3},{5,4},{6,5},{7,6},{9,8},{10,9},{11,10},{12... | collective-permute-start | bytes 315800 | tf_op jit(solution)/shard_map/ppermute | solution.py:31
  570.3 4.1 collective-permute-done.16
  584.6 3.9 collective-permute-start.20
  589.2 4.0 collective-permute-done.21
  593.2 15.2 %collective-permute-done.20 = f32[3,4,34,1]{3,1,2,0:T(4,128)S(1)} collective-permute-done((f32[3,4,34,1]{3,1,2,0:T(4,128)S(1)}, f32[3,4,34,1]{3,1,2,0:T(4,128)S(1)}, u32[]{:S(2)}, u32[]{:S(2)}) %collective-permute-start.20) | collective-permute-done | bytes 1664 | tf_op jit(solution)/shard_map/ppermute | solution.py:30
  609.1 12.2 %collective-permute-start.23 = (f32[3,1,34,258]{3,2,1,0:T(8,128)S(1)}, f32[3,1,34,258]{3,2,1,0:T(8,128)S(1)}, u32[]{:S(2)}, u32[]{:S(2)}) collective-permute-start(f32[3,1,34,258]{3,2,1,0:T(8,128)S(1)} %get-tuple-element.92), channel_id=1, source_target_pairs={{1,0},{2,1},{3,2},{4,3},{5,4},{6,5},{7,6},{9,8},{10,9},{11,10},{12... | collective-permute-start | bytes 315800 | tf_op jit(solution)/shard_map/ppermute | solution.py:31
  625.4 4.1 collective-permute-done.22
  (640 shorter events, 365.7 us)
Async XLA Ops:
  46.3 287.5 %all-to-all-start = ((bf16[8,3,2,16,128]{4,3,2,1,0:T(8,128)(2,1)}), bf16[8,3,2,16,128]{4,3,2,1,0:T(8,128)(2,1)S(1)}, u32[]{:S(2)}, u32[]{:S(2)}) async-start(bf16[8,3,2,16,128]{4,3,2,1,0:T(8,128)(2,1)} %stack.14), calls=%async_computation | async-start | bytes 393216 | tf_op jit(solution)/shard_map/all_to_all | solution.py:13
  51.1 376.7 %all-gather.3.cloned.1.call-start = ((), (), s32[]{:S(2)}) async-start(), calls=%async_computation.1 | async-start | bytes 1769472 | tf_op jit(solution)/shard_map/all_gather | solution.py:124
  51.1 407.4 %collective-permute-start.7 = (f32[3,4,1,256]{3,1,2,0:T(4,128)S(1)}, f32[3,4,1,256]{3,1,2,0:T(4,128)S(1)}, u32[]{:S(2)}, u32[]{:S(2)}) collective-permute-start(f32[3,4,1,256]{3,1,2,0:T(4,128)S(1)} %copy.557), channel_id=1, source_target_pairs={{64,0},{128,64},{192,128},{256,192},{320,256},{384,320},{448,384},... | collective-permute-start | bytes 36872 | tf_op jit(solution)/shard_map/ppermute | solution.py:31
  53.2 405.1 %collective-permute-start.6 = (f32[3,4,1,256]{3,1,2,0:T(4,128)S(1)}, f32[3,4,1,256]{3,1,2,0:T(4,128)S(1)}, u32[]{:S(2)}, u32[]{:S(2)}) collective-permute-start(f32[3,4,1,256]{3,1,2,0:T(4,128)S(1)} %copy.558), channel_id=1, source_target_pairs={{0,64},{64,128},{128,192},{192,256},{256,320},{320,384},{384,448},... | collective-permute-start | bytes 36872 | tf_op jit(solution)/shard_map/ppermute | solution.py:30
  55.5 376.6 %collective-permute-start = (bf16[1,4,1,256]{3,2,1,0:T(2,128)(2,1)S(1)}, bf16[1,4,1,256]{3,2,1,0:T(2,128)(2,1)S(1)}, u32[]{:S(2)}, u32[]{:S(2)}) collective-permute-start(bf16[1,4,1,256]{3,2,1,0:T(2,128)(2,1)S(1)} %get-tuple-element.126), channel_id=1, source_target_pairs={{0,64},{64,128},{128,192},{192,256},{256,320},{320,384},{384,448},... | collective-permute-start | bytes 6152 | tf_op jit(solution)/shard_map/ppermute | solution.py:30
  58.8 373.4 %collective-permute-start.1 = (bf16[1,4,1,256]{3,2,1,0:T(2,128)(2,1)S(1)}, bf16[1,4,1,256]{3,2,1,0:T(2,128)(2,1)S(1)}, u32[]{:S(2)}, u32[]{:S(2)}) collective-permute-start(bf16[1,4,1,256]{3,2,1,0:T(2,128)(2,1)S(1)} %get-tuple-element.125), channel_id=1, source_target_pairs={{64,0},{128,64},{192,128},{256,192},{320,256},{384,320},{448,384},... | collective-permute-start | bytes 6152 | tf_op jit(solution)/shard_map/ppermute | solution.py:31
  334.7 177.8 %all-gather.5.cloned.1.call-start = ((), (), s32[]{:S(2)}) async-start(), calls=%async_computation.2 | async-start | bytes 1769472 | tf_op jit(solution)/shard_map/all_gather | solution.py:135
  432.3 9.6 %collective-permute-start.3 = (bf16[1,4,34,1]{3,1,2,0:T(4,128)(2,1)S(1)}, bf16[1,4,34,1]{3,1,2,0:T(4,128)(2,1)S(1)}, u32[]{:S(2)}, u32[]{:S(2)}) collective-permute-start(bf16[1,4,34,1]{3,1,2,0:T(4,128)(2,1)S(1)} %get-tuple-element.124), channel_id=1, source_target_pairs={{8,0},{16,8},{24,16},{32,24},{40,32},{48,40},{56,48},{9,1},{17,9},... | collective-permute-start | bytes 824 | tf_op jit(solution)/shard_map/ppermute | solution.py:31
  439.9 18.2 %collective-permute-start.2 = (bf16[1,4,34,1]{3,1,2,0:T(4,128)(2,1)S(1)}, bf16[1,4,34,1]{3,1,2,0:T(4,128)(2,1)S(1)}, u32[]{:S(2)}, u32[]{:S(2)}) collective-permute-start(bf16[1,4,34,1]{3,1,2,0:T(4,128)(2,1)S(1)} %get-tuple-element.123), channel_id=1, source_target_pairs={{0,8},{8,16},{16,24},{24,32},{32,40},{40,48},{48,56},{1,9},{9,17},... | collective-permute-start | bytes 824 | tf_op jit(solution)/shard_map/ppermute | solution.py:30
  458.8 18.8 %collective-permute-start.9 = (f32[3,4,34,1]{3,1,2,0:T(4,128)S(1)}, f32[3,4,34,1]{3,1,2,0:T(4,128)S(1)}, u32[]{:S(2)}, u32[]{:S(2)}) collective-permute-start(f32[3,4,34,1]{3,1,2,0:T(4,128)S(1)} %get-tuple-element.108), channel_id=1, source_target_pairs={{8,0},{16,8},{24,16},{32,24},{40,32},{48,40},{56,48},{9,1},{17,9},... | collective-permute-start | bytes 4904 | tf_op jit(solution)/shard_map/ppermute | solution.py:31
  460.7 31.4 %collective-permute-start.8 = (f32[3,4,34,1]{3,1,2,0:T(4,128)S(1)}, f32[3,4,34,1]{3,1,2,0:T(4,128)S(1)}, u32[]{:S(2)}, u32[]{:S(2)}) collective-permute-start(f32[3,4,34,1]{3,1,2,0:T(4,128)S(1)} %get-tuple-element.107), channel_id=1, source_target_pairs={{0,8},{8,16},{16,24},{24,32},{32,40},{40,48},{48,56},{1,9},{9,17},... | collective-permute-start | bytes 4904 | tf_op jit(solution)/shard_map/ppermute | solution.py:30
  464.7 46.6 %collective-permute-start.5 = (bf16[1,1,34,258]{3,2,1,0:T(8,128)(2,1)S(1)}, bf16[1,1,34,258]{3,2,1,0:T(8,128)(2,1)S(1)}, u32[]{:S(2)}, u32[]{:S(2)}) collective-permute-start(bf16[1,1,34,258]{3,2,1,0:T(8,128)(2,1)S(1)} %copy.559), channel_id=1, source_target_pairs={{1,0},{2,1},{3,2},{4,3},{5,4},{6,5},{7,6},{9,8},{10,9},{11,10},{12... | collective-permute-start | bytes 52640 | tf_op jit(solution)/shard_map/ppermute | solution.py:31
  467.6 43.8 %collective-permute-start.4 = (bf16[1,1,34,258]{3,2,1,0:T(8,128)(2,1)S(1)}, bf16[1,1,34,258]{3,2,1,0:T(8,128)(2,1)S(1)}, u32[]{:S(2)}, u32[]{:S(2)}) collective-permute-start(bf16[1,1,34,258]{3,2,1,0:T(8,128)(2,1)S(1)} %copy.560), channel_id=1, source_target_pairs={{0,1},{1,2},{2,3},{3,4},{4,5},{5,6},{6,7},{8,9},{9,10},{10,11},{11... | collective-permute-start | bytes 52640 | tf_op jit(solution)/shard_map/ppermute | solution.py:30
  493.5 25.9 %collective-permute-start.11 = (f32[3,1,34,258]{3,2,1,0:T(8,128)}, f32[3,1,34,258]{3,2,1,0:T(8,128)}, u32[]{:S(2)}, u32[]{:S(2)}) collective-permute-start(f32[3,1,34,258]{3,2,1,0:T(8,128)} %get-tuple-element.96), channel_id=1, source_target_pairs={{1,0},{2,1},{3,2},{4,3},{5,4},{6,5},{7,6},{9,8},{10,9},{11,10},{12... | collective-permute-start | bytes 315800 | tf_op jit(solution)/shard_map/ppermute | solution.py:31
  508.0 11.4 %collective-permute-start.10 = (f32[3,1,34,258]{3,2,1,0:T(8,128)}, f32[3,1,34,258]{3,2,1,0:T(8,128)}, u32[]{:S(2)}, u32[]{:S(2)}) collective-permute-start(f32[3,1,34,258]{3,2,1,0:T(8,128)} %get-tuple-element.95), channel_id=1, source_target_pairs={{0,1},{1,2},{2,3},{3,4},{4,5},{5,6},{6,7},{8,9},{9,10},{10,11},{11... | collective-permute-start | bytes 315800 | tf_op jit(solution)/shard_map/ppermute | solution.py:30
  529.0 9.3 %collective-permute-start.15 = (f32[3,4,34,1]{3,1,2,0:T(4,128)S(1)}, f32[3,4,34,1]{3,1,2,0:T(4,128)S(1)}, u32[]{:S(2)}, u32[]{:S(2)}) collective-permute-start(f32[3,4,34,1]{3,1,2,0:T(4,128)S(1)} %get-tuple-element.104), channel_id=1, source_target_pairs={{8,0},{16,8},{24,16},{32,24},{40,32},{48,40},{56,48},{9,1},{17,9},... | collective-permute-start | bytes 4904 | tf_op jit(solution)/shard_map/ppermute | solution.py:31
  530.9 20.4 %collective-permute-start.14 = (f32[3,4,34,1]{3,1,2,0:T(4,128)S(1)}, f32[3,4,34,1]{3,1,2,0:T(4,128)S(1)}, u32[]{:S(2)}, u32[]{:S(2)}) collective-permute-start(f32[3,4,34,1]{3,1,2,0:T(4,128)S(1)} %get-tuple-element.103), channel_id=1, source_target_pairs={{0,8},{8,16},{16,24},{24,32},{32,40},{40,48},{48,56},{1,9},{9,17},... | collective-permute-start | bytes 4904 | tf_op jit(solution)/shard_map/ppermute | solution.py:30
  552.0 18.3 %collective-permute-start.17 = (f32[3,1,34,258]{3,2,1,0:T(8,128)S(1)}, f32[3,1,34,258]{3,2,1,0:T(8,128)S(1)}, u32[]{:S(2)}, u32[]{:S(2)}) collective-permute-start(f32[3,1,34,258]{3,2,1,0:T(8,128)S(1)} %get-tuple-element.94), channel_id=1, source_target_pairs={{1,0},{2,1},{3,2},{4,3},{5,4},{6,5},{7,6},{9,8},{10,9},{11,10},{12... | collective-permute-start | bytes 315800 | tf_op jit(solution)/shard_map/ppermute | solution.py:31
  566.2 8.2 %collective-permute-start.16 = (f32[3,1,34,258]{3,2,1,0:T(8,128)S(1)}, f32[3,1,34,258]{3,2,1,0:T(8,128)S(1)}, u32[]{:S(2)}, u32[]{:S(2)}) collective-permute-start(f32[3,1,34,258]{3,2,1,0:T(8,128)S(1)} %get-tuple-element.93), channel_id=1, source_target_pairs={{0,1},{1,2},{2,3},{3,4},{4,5},{5,6},{6,7},{8,9},{9,10},{10,11},{11... | collective-permute-start | bytes 315800 | tf_op jit(solution)/shard_map/ppermute | solution.py:30
  575.5 5.6 collective-permute-start.18
  582.7 10.6 %collective-permute-start.21 = (f32[3,4,34,1]{3,1,2,0:T(4,128)S(1)}, f32[3,4,34,1]{3,1,2,0:T(4,128)S(1)}, u32[]{:S(2)}, u32[]{:S(2)}) collective-permute-start(f32[3,4,34,1]{3,1,2,0:T(4,128)S(1)} %get-tuple-element.100), channel_id=1, source_target_pairs={{8,0},{16,8},{24,16},{32,24},{40,32},{48,40},{56,48},{9,1},{17,9},... | collective-permute-start | bytes 4904 | tf_op jit(solution)/shard_map/ppermute | solution.py:31
  584.6 23.9 %collective-permute-start.20 = (f32[3,4,34,1]{3,1,2,0:T(4,128)S(1)}, f32[3,4,34,1]{3,1,2,0:T(4,128)S(1)}, u32[]{:S(2)}, u32[]{:S(2)}) collective-permute-start(f32[3,4,34,1]{3,1,2,0:T(4,128)S(1)} %get-tuple-element.99), channel_id=1, source_target_pairs={{0,8},{8,16},{16,24},{24,32},{32,40},{40,48},{48,56},{1,9},{9,17},... | collective-permute-start | bytes 4904 | tf_op jit(solution)/shard_map/ppermute | solution.py:30
  609.1 16.3 %collective-permute-start.23 = (f32[3,1,34,258]{3,2,1,0:T(8,128)S(1)}, f32[3,1,34,258]{3,2,1,0:T(8,128)S(1)}, u32[]{:S(2)}, u32[]{:S(2)}) collective-permute-start(f32[3,1,34,258]{3,2,1,0:T(8,128)S(1)} %get-tuple-element.92), channel_id=1, source_target_pairs={{1,0},{2,1},{3,2},{4,3},{5,4},{6,5},{7,6},{9,8},{10,9},{11,10},{12... | collective-permute-start | bytes 315800 | tf_op jit(solution)/shard_map/ppermute | solution.py:31
  621.3 8.3 %collective-permute-start.22 = (f32[3,1,34,258]{3,2,1,0:T(8,128)S(1)}, f32[3,1,34,258]{3,2,1,0:T(8,128)S(1)}, u32[]{:S(2)}, u32[]{:S(2)}) collective-permute-start(f32[3,1,34,258]{3,2,1,0:T(8,128)S(1)} %get-tuple-element.91), channel_id=1, source_target_pairs={{0,1},{1,2},{2,3},{3,4},{4,5},{5,6},{6,7},{8,9},{9,10},{10,11},{11... | collective-permute-start | bytes 315800 | tf_op jit(solution)/shard_map/ppermute | solution.py:30
  (14 other events, 747.3 us)
Sparse Core Ops, SparseCore 0:
  334.8 92.9 all-gather.2
  432.2 70.8 all-gather.4
